TPU v7x, 32 devices: a whole 2x2x4 slice. The times are simulated.
32 devices in a mesh: gx: 4 (over z), gy: 8 (over y, x, core).
Axes of the slice: x: 2, y: 2, z: 4, core: 2. Of those that a mesh axis runs over, the one named last changes fastest.
Arguments:
- particles: bfloat16 [2048, 4096], P(('gx', 'gy')), may hold values from -6 to 6
- references: bfloat16 [4, 12, 4096], P('gx'), may hold values from -1 to 1
- slot_class: int32 [4], replicated, may hold values from 0 to 3, each once
- log_prior: float32 [4], replicated, may hold values from -2 to 2
- shift_offsets: int32 [8, 2], replicated, may hold values from -8 to 8
- group_ids: int32 [2048], P(('gx', 'gy')), may hold values from 0 to 127
- ctf_table: float32 [128, 2048], replicated, may hold values from -1 to 1
- noise_power: float32 [2048], replicated, may hold values from 0.5 to 2
Outputs:
- class_sums: float32 [4, 12, 4096], P('gx')
- ctf_power: float32 [4, 2048], P('gx')
- log_evidence: float32 [], replicated
Inputs may be any that keep to these rules, and one draw needn't show every extreme that they name: `slot_class`: each class id stands at exactly one slot.
All inputs are finite; a program needn't handle non-finite values.
Results may differ from a plain program's by a relative error of at most 0.006.
Values may be sent and summed in bfloat16 or wider, within the bound.
No kernel may reach another device: no remote copies, remote signals or barrier semaphores. Data moves between devices by JAX's collectives and lax.ppermute only.
A program may use at most 64 MiB of HBM per device.

v0:
```python
import jax
import jax.numpy as jnp
from jax import lax
from jax.sharding import PartitionSpec as P

L = 64
R = 12
NS = 8
G = 128
HALF = 2048
FR = 4096


def phase_tables(shift_offsets, edge_len):
    half_size = edge_len * edge_len // 2
    freq_index = jnp.arange(half_size, dtype=jnp.int32)
    row_freq = freq_index // (edge_len // 2)
    col_freq = freq_index % (edge_len // 2)
    phase_turns = jnp.mod(
        row_freq[None, :] * shift_offsets[:, 0:1] + col_freq[None, :] * shift_offsets[:, 1:2],
        edge_len,
    )
    angles = phase_turns.astype(jnp.float32) * (2.0 * jnp.pi / edge_len)
    return (jnp.cos(angles), jnp.sin(angles))


def spectra(particles, edge_len):
    rows_here = particles.shape[0]
    half_side = edge_len // 2
    images = particles.astype(jnp.float32).reshape(rows_here * edge_len, edge_len)
    pixel_index = jnp.arange(edge_len, dtype=jnp.int32)
    column_turns = jnp.mod(pixel_index[:, None] * pixel_index[None, :half_side], edge_len).astype(
        jnp.float32
    ) * (2.0 * jnp.pi / edge_len)
    column_table = jnp.concatenate([jnp.cos(column_turns), -jnp.sin(column_turns)], axis=1)
    partial_x = jnp.dot(
        images, column_table, precision=lax.Precision.HIGHEST, preferred_element_type=jnp.float32
    )
    partial_x = partial_x.reshape(rows_here, edge_len, edge_len)
    row_turns = jnp.mod(pixel_index[:, None] * pixel_index[None, :], edge_len).astype(
        jnp.float32
    ) * (2.0 * jnp.pi / edge_len)
    with_cos = jnp.einsum(
        "uy,pyw->puw", jnp.cos(row_turns), partial_x, precision=lax.Precision.HIGHEST
    )
    with_sin = jnp.einsum(
        "uy,pyw->puw", jnp.sin(row_turns), partial_x, precision=lax.Precision.HIGHEST
    )
    real_part = (with_cos[..., :half_side] + with_sin[..., half_side:]) / edge_len
    imag_part = (with_cos[..., half_side:] - with_sin[..., :half_side]) / edge_len
    return (real_part.reshape(rows_here, -1), imag_part.reshape(rows_here, -1))


def shards(
    particles, references, slot_class, log_prior, shift_offsets, group_ids, ctf_table, noise_power
):
    rows_here = particles.shape[0]
    classes = lax.axis_size("gx") * references.shape[0]
    row_width = R * NS
    real_part, imag_part = spectra(particles, L)
    inv_noise = 1.0 / noise_power
    group_hot = (group_ids[:, None] == jnp.arange(G, dtype=jnp.int32)[None, :]).astype(jnp.float32)
    ctf_rows = jnp.dot(
        group_hot, ctf_table, precision=lax.Precision.HIGHEST, preferred_element_type=jnp.float32
    )
    whiten = ctf_rows * inv_noise
    weighted = jnp.concatenate([real_part * whiten, imag_part * whiten], axis=1).astype(
        jnp.bfloat16
    )
    data_power = jnp.sum((real_part * real_part + imag_part * imag_part) * inv_noise, axis=1)
    cosines, sine_table = phase_tables(shift_offsets, L)
    power_table = ctf_table * ctf_table * inv_noise
    blank = jnp.zeros((rows_here, classes * row_width), jnp.float32)
    piece = lax.all_gather(references, "gx", axis=0, tiled=True)

    def add_class(offset, table):
        stack_row = lax.dynamic_index_in_dim(piece, offset, 0, keepdims=False).astype(jnp.float32)
        stack_real = stack_row[:, :HALF]
        stack_imag = stack_row[:, HALF:]
        shifted_real = (
            stack_real[:, None, :] * cosines[None] + stack_imag[:, None, :] * sine_table[None]
        )
        shifted_imag = (
            stack_imag[:, None, :] * cosines[None] - stack_real[:, None, :] * sine_table[None]
        )
        shifted = (
            jnp.concatenate([shifted_real, shifted_imag], axis=2)
            .astype(jnp.bfloat16)
            .reshape(row_width, FR)
        )
        intersection = lax.dot_general(
            weighted, shifted, (((1,), (1,)), ((), ())), preferred_element_type=jnp.float32
        )
        amplitude = stack_real * stack_real + stack_imag * stack_imag
        ref_power = jnp.dot(
            power_table,
            amplitude.T,
            precision=lax.Precision.HIGHEST,
            preferred_element_type=jnp.float32,
        )
        own_power = jnp.dot(
            group_hot,
            ref_power,
            precision=lax.Precision.HIGHEST,
            preferred_element_type=jnp.float32,
        )
        logits = intersection.reshape(rows_here, R, NS) - 0.5 * own_power[:, :, None]
        return lax.dynamic_update_slice_in_dim(
            table, logits.reshape(rows_here, row_width), offset * row_width, 1
        )

    scores = lax.fori_loop(0, piece.shape[0], add_class, blank)
    slot_prior = jnp.sum(
        jnp.where(
            slot_class[:, None] == jnp.arange(classes, dtype=jnp.int32)[None, :],
            log_prior[None, :],
            0.0,
        ),
        axis=1,
    )
    logits = (
        scores.reshape(rows_here, classes, row_width)
        - 0.5 * data_power[:, None, None]
        + slot_prior[None, :, None]
    )
    row_max = jnp.max(logits, axis=(1, 2), keepdims=True)
    raised = jnp.exp(logits - row_max)
    normaliser = jnp.sum(raised, axis=(1, 2), keepdims=True)
    weights = raised / normaliser
    evidence = row_max[:, 0, 0] + jnp.log(normaliser[:, 0, 0])
    weights_low = weights.astype(jnp.bfloat16)
    group_weights = jnp.dot(
        jnp.sum(weights, axis=2).T,
        group_hot,
        precision=lax.Precision.HIGHEST,
        preferred_element_type=jnp.float32,
    )

    def class_terms(slot_index):
        weight_cols = lax.dynamic_index_in_dim(weights_low, slot_index, 1, keepdims=False)
        moment = lax.dot_general(
            weight_cols, weighted, (((0,), (0,)), ((), ())), preferred_element_type=jnp.float32
        )
        moment = moment.reshape(R, NS, FR)
        moment_real = moment[..., :HALF]
        moment_imag = moment[..., HALF:]
        back_real = jnp.sum(moment_real * cosines[None] - moment_imag * sine_table[None], axis=1)
        back_imag = jnp.sum(moment_imag * cosines[None] + moment_real * sine_table[None], axis=1)
        return jnp.concatenate([back_real, back_imag], axis=1)

    owned = lax.psum_scatter(
        lax.map(
            lambda offset: class_terms(offset),
            jnp.arange(references.shape[0] * lax.axis_size("gx"), dtype=jnp.int32),
        ),
        "gx",
        scatter_dimension=0,
        tiled=True,
    )
    class_sums = lax.psum(owned, "gy")
    totals, evidence_sum = lax.psum((group_weights, jnp.sum(evidence)), ("gx", "gy"))
    own_groups = lax.dynamic_slice_in_dim(totals, lax.axis_index("gx"), 1, 0)
    ctf_power = jnp.dot(
        own_groups,
        ctf_table * ctf_table,
        precision=lax.Precision.HIGHEST,
        preferred_element_type=jnp.float32,
    )
    log_evidence = evidence_sum / (rows_here * lax.axis_size("gx") * lax.axis_size("gy") * HALF)
    return (class_sums, ctf_power, log_evidence)


def solution(mesh):
    return jax.shard_map(
        shards,
        mesh=mesh,
        in_specs=(
            P(("gx", "gy"), None),
            P("gx", None, None),
            P(),
            P(),
            P(),
            P(("gx", "gy")),
            P(),
            P(),
        ),
        out_specs=(P("gx", None, None), P("gx", None), P()),
        check_vma=False,
    )
```

profile of v0, /device:TPU:0, one launch (start us, length us, event | category | flops | bytes accessed | tf_op | source)
XLA Modules:
  0.0 206.5 jit_solution(13460478304987082292)
XLA Ops:
  7.4 2.1 reshape.111
  9.4 1.3 convolution_bitcast_fusion.1
  11.6 4.6 %fusion.46 = f32[64,64,64]{1,2,0:T(8,128)} fusion(f32[64,64,64]{1,0,2:T(8,128)S(1)} %reshape.112), kind=kOutput, calls=%fused_computation.59 | convolution fusion | flops 201383936 | bytes 2097152 | tf_op jit(solution)/shard_map/uy,pyw->puw/dot_general | solution.py:43
  16.2 4.7 %fusion.49 = f32[64,64,64]{1,2,0:T(8,128)} fusion(f32[64,64,64]{1,0,2:T(8,128)S(1)} %reshape.112), kind=kOutput, calls=%fused_computation.60 | convolution fusion | flops 201383936 | bytes 2097152 | tf_op jit(solution)/shard_map/uy,pyw->puw/dot_general | solution.py:46
  21.7 3.4 %multiply_reduce_fusion = (f32[64]{0:T(128)}, f32[64,64,32]{1,2,0:T(8,128)S(1)}, f32[64,64,32]{1,2,0:T(8,128)S(1)}) fusion(f32[64,32]{0,1:T(8,128)S(1)} %copy.44, f32[64,64,64]{1,2,0:T(8,128)} %fusion.49, f32[64,64,64]{1,2,0:T(8,128)} %fusion.46), kind=kLoop, calls=%fused_computation.65 | loop fusion | flops 1179584 | bytes 3154176 | tf_op jit(solution)/shard_map/reduce_sum | solution.py:70
  25.1 1.1 copy.39
  26.1 1.1 copy.40
  27.3 1.1 copy.41
  28.4 1.1 copy.42
  30.3 18.2 %all_gather.3 = bf16[4,12,4096]{2,1,0:T(8,128)(2,1)} all-gather(bf16[1,12,4096]{2,1,0:T(8,128)(2,1)S(1)} %copy-done.3), channel_id=1, replica_groups=mesh['gx'=4,'gy'=8] {'gx'}, dimensions={0}, use_global_device_ids=true | all-gather | bytes 491520 | tf_op jit(solution)/shard_map/all_gather | solution.py:74
  48.4 1.2 multiply_convert_fusion.1
  49.7 25.9 %while.27 = (s32[]{:T(128)}, f32[64,384]{1,0:T(8,128)S(1)}, bf16[4,12,4096]{2,1,0:T(8,128)(2,1)}, bf16[64,4096]{1,0:T(8,128)(2,1)S(1)}, f32[128,2048]{1,0:T(8,12...) while((s32[]{:T(128)}, f32[64,384]{1,0:T(8,128)S(1)}, ...), condition=%wide.region_1.2_spmd.clone.clone, body=%wide.region_0.1_spmd.clone.clone.sunk | while | flops 92814080 | bytes 4696571 | solution.py:112
  50.7 1.1 fusion.137
  54.5 1.2 fusion.140
  57.1 1.1 fusion.137
  60.9 1.2 fusion.140
  63.6 1.1 fusion.137
  67.4 1.2 fusion.140
  74.0 1.2 fusion.140
  78.0 21.0 %while.28 = (s32[]{:T(128)}, f32[4,12,4096]{2,1,0:T(8,128)}, s32[4]{0:T(128)S(1)}, bf16[64,4,96]{0,2,1:T(8,128)(2,1)S(1)}, bf16[64,4096]{1,0:T(8,128)(2,1)S(1)},...) while((s32[]{:T(128)}, f32[4,12,4096]{2,1,0:T(8,128)}, ...), condition=%wide.region_9.10_spmd.clone.clone, body=%wide.region_6.9_spmd.clone.clone.sunk | while | flops 52166660 | bytes 4629223 | solution.py:152
  100.5 42.4 %all-reduce = (f32[4,128]{1,0:T(4,128)S(1)}, f32[]{:T(128)}) all-reduce(f32[4,128]{1,0:T(4,128)S(1)} %fusion.68, f32[]{:T(128)} %add_reduce_fusion.1), channel_id=1, replica_groups=mesh['gx'=4,'gy'=8] {'gx','gy'}, use_global_device_ids=true, to_apply=%region_13.14 | all-reduce | flops 513 | bytes 4104 | tf_op jit(solution)/shard_map/psum | solution.py:161
  143.0 1.2 fusion.54
  144.9 51.8 %all-reduce.3.cloned.1.call-done = f32[1,12,4096]{2,1,0:T(8,128)} async-done(((f32[1,12,4096]{2,1,0:T(8,128)}), f32[1,12,4096]{2,1,0:T(8,128)}) %all-reduce.3.cloned.1.call-update) | async-done | bytes 196624 | tf_op jit(solution)/shard_map/psum | solution.py:160
  196.7 1.8 copy.45
  (93 shorter events, 37.4 us)
Async XLA Ops:
  7.2 135.8 %reduce-scatter.2.cloned.1.call-start = ((), (), s32[]{:S(2)}) async-start(), calls=%async_computation.1 | async-start | bytes 1310720 | tf_op jit(solution)/shard_map/reduce_scatter | solution.py:151
  16.2 5.3 %copy-start.4 = (f32[2048]{0:T(1024)S(1)}, f32[2048]{0:T(1024)}, u32[]{:S(2)}) copy-start(f32[2048]{0:T(1024)} %param.19) | copy-start | bytes 24580
  27.3 2.3 %copy-start = (f32[128,2048]{1,0:T(8,128)S(1)}, f32[128,2048]{1,0:T(8,128)}, u32[]{:S(2)}) copy-start(f32[128,2048]{1,0:T(8,128)} %param.18) | copy-start | bytes 3145732
  28.4 1.3 copy-start.5
  28.4 1.9 copy-start.3
  29.5 18.9 %copy-start.1 = (f32[64,2048]{1,0:T(8,128)S(1)}, f32[64,2048]{1,0:T(8,128)}, u32[]{:S(2)}) copy-start(f32[64,2048]{1,0:T(8,128)} %copy.40) | copy-start | bytes 1572868
  29.5 18.9 %copy-start.2 = (f32[64,2048]{1,0:T(8,128)S(1)}, f32[64,2048]{1,0:T(8,128)}, u32[]{:S(2)}) copy-start(f32[64,2048]{1,0:T(8,128)} %copy.42) | copy-start | bytes 1572868
  99.0 97.7 %all-reduce.3.cloned.1.call-start = ((), (), s32[]{:S(2)}) async-start(), calls=%async_computation.2 | async-start | bytes 524288 | tf_op jit(solution)/shard_map/psum | solution.py:160
Sparse Core Ops, SparseCore 0:
  99.2 29.8 reduce-scatter.1
  143.1 53.5 all-reduce.2
where the time goes:
time: 208 us; the launch traced here: 206 us
  blocking collectives  60.6 us (29%)
  waiting for transfers between devices  51.9 us (25%)
  matrix products  27.2 us (13%)
  other arithmetic  25.1 us (12%)
  local copies, waits for them, and re-layouts  17.6 us (8%)
  between operations  16 us (8%)
  loops' own time  8.13 us (4%)
    psum x1, waiting for transfers between devices, shards(): class_sums = lax.psum(owned, 'gy')  51.8 us
    psum x1, blocking collectives, shards(): lax.psum((group_weights, jnp.sum(evidence)), ('gx', 'gy'))  42.4 us
    all_gather x1, blocking collectives, shards(): piece = lax.all_gather(references, 'gx', axis=0, tiled=True)  18.2 us
    cos x8, other arithmetic, phase_tables(): return (jnp.cos(angles), jnp.sin(angles))  8.53 us
    another operation x1, loops' own time, shards(): lax.map(lambda offset: class_terms(offset), jnp.arange(references.shape[0...  7.85 us
    dot_general x1, matrix products, spectra(): jnp.einsum('uy,pyw->puw', jnp.sin(row_turns), partial_x, precision=lax.Pr...  4.7 us
    dot_general x1, matrix products, spectra(): jnp.einsum('uy,pyw->puw', jnp.cos(row_turns), partial_x, precision=lax.Pr...  4.65 us
    dot_general x4, matrix products, add_class(): lax.dot_general(weighted, shifted, (((1,), (1,)), ((), ())), preferred_el...  4.62 us
  transfers between devices with their start and end apart: 2, of which 1 were waited for; matrix products, arithmetic and copies ran while one was open for 1% of the time, Pallas kernels for 0%

commit v1 on v0

--- a/solution.py
+++ b/solution.py
@@ -2,6 +2,7 @@
 import jax.numpy as jnp
 from jax import lax
 from jax.sharding import PartitionSpec as P
+from jax.lax import axis_index, ppermute, psum
 
 L = 64
 R = 12
@@ -71,7 +72,19 @@
     cosines, sine_table = phase_tables(shift_offsets, L)
     power_table = ctf_table * ctf_table * inv_noise
     blank = jnp.zeros((rows_here, classes * row_width), jnp.float32)
-    piece = lax.all_gather(references, "gx", axis=0, tiled=True)
+    devs = psum(1, "gx")
+    line_up = [(d, (d + 1) % devs) for d in range(devs)]
+    pieces_in = [(d, (d - 1) % devs) for d in range(devs)]
+    f_next, step_out = ([references], [references])
+    for _ in range(devs // 2):
+        base_arr = ppermute(f_next[-1], "gx", line_up)
+        f_next.append(base_arr)
+    for _ in tuple(range((devs - 1) // 2)):
+        kept_arr = ppermute(step_out[-1], "gx", pieces_in)
+        step_out.append(kept_arr)
+    parts_out = jnp.concatenate([*f_next[::-1], *step_out[1:]], axis=0)
+    reply = axis_index("gx")
+    piece = jnp.roll(parts_out, shift=(reply - devs // 2) * references.shape[0], axis=0)
 
     def add_class(offset, table):
         stack_row = lax.dynamic_index_in_dim(piece, offset, 0, keepdims=False).astype(jnp.float32)

time: 208 us -> 201 us (0.966)
  blocking collectives: 60.6 us -> 39.2 us
  waiting for transfers between devices: 51.9 us -> 58.5 us
  starting transfers between devices: 0.08 us -> 5.28 us
    all_gather x1 -> x0, blocking collectives: 18.2 us -> none  [shards(): piece = lax.all_gather(references, 'gx', axis=0, tiled=True)]
    ppermute x0 -> x3, waiting for transfers between devices: none -> 6.16 us  [the longest x2 6.16 us: shards(): base_arr = ppermute(f_next[-1], 'gx', line_up)]
    ppermute x0 -> x3, starting transfers between devices: none -> 5.2 us  [the longest x2 3.11 us: shards(): base_arr = ppermute(f_next[-1], 'gx', line_up)]
    psum x1, blocking collectives: 42.4 us -> 39.2 us  [shards(): lax.psum((group_weights, jnp.sum(evidence)), ('gx', 'gy'))]
  transfers between devices with their start and end apart: 2 -> 5, of which waited for: 1 -> 2; matrix products, arithmetic and copies ran while one was open for 1% -> 14% of each run, Pallas kernels for 0% -> 0%
where the time goes in v1:
time: 201 us; the launch traced here: 199 us
  waiting for transfers between devices  58.5 us (29%)
  blocking collectives  39.2 us (20%)
  matrix products  27.4 us (14%)
  other arithmetic  25.7 us (13%)
  local copies, waits for them, and re-layouts  19.1 us (10%)
  between operations  16.1 us (8%)
  loops' own time  8.12 us (4%)
  starting transfers between devices  5.28 us (3%)
    psum x1, waiting for transfers between devices, shards(): class_sums = lax.psum(owned, 'gy')  52.3 us
    psum x1, blocking collectives, shards(): lax.psum((group_weights, jnp.sum(evidence)), ('gx', 'gy'))  39.2 us
    cos x8, other arithmetic, phase_tables(): return (jnp.cos(angles), jnp.sin(angles))  8.53 us
    another operation x1, loops' own time, shards(): lax.map(lambda offset: class_terms(offset), jnp.arange(references.shape[0...  7.85 us
    ppermute x2, waiting for transfers between devices, shards(): base_arr = ppermute(f_next[-1], 'gx', line_up)  6.16 us
    dot_general x1, matrix products, spectra(): jnp.einsum('uy,pyw->puw', jnp.sin(row_turns), partial_x, precision=lax.Pr...  4.7 us
    dot_general x1, matrix products, spectra(): jnp.einsum('uy,pyw->puw', jnp.cos(row_turns), partial_x, precision=lax.Pr...  4.65 us
    dot_general x4, matrix products, add_class(): lax.dot_general(weighted, shifted, (((1,), (1,)), ((), ())), preferred_el...  4.62 us
  transfers between devices with their start and end apart: 5, of which 2 were waited for; matrix products, arithmetic and copies ran while one was open for 14% of the time, Pallas kernels for 0%

profile of v1, /device:TPU:0, one launch (start us, length us, event | category | flops | bytes accessed | tf_op | source)
XLA Modules:
  0.0 199.4 jit_solution(4063208097756381915)
XLA Ops:
  7.2 3.1 %collective-permute-start = (bf16[1,12,4096]{2,1,0:T(8,128)(2,1)}, bf16[1,12,4096]{2,1,0:T(8,128)(2,1)S(1)}, u32[]{:S(2)}, u32[]{:S(2)}) collective-permute-start(bf16[1,12,4096]{2,1,0:T(8,128)(2,1)} %param.13), channel_id=1, source_target_pairs={{0,8},{8,16},{16,24},{24,0},{1,9},{9,17},{17,25},{25,1},{2,10},{10... | collective-permute-start | bytes 294920 | tf_op jit(solution)/shard_map/ppermute | solution.py:80
  10.3 2.1 %collective-permute-start.2 = (bf16[1,12,4096]{2,1,0:T(8,128)(2,1)}, bf16[1,12,4096]{2,1,0:T(8,128)(2,1)S(1)}, u32[]{:S(2)}, u32[]{:S(2)}) collective-permute-start(bf16[1,12,4096]{2,1,0:T(8,128)(2,1)} %param.13), channel_id=1, source_target_pairs={{0,24},{8,0},{16,8},{24,16},{1,25},{9,1},{17,9},{25,17},{2,26},{10... | collective-permute-start | bytes 294920 | tf_op jit(solution)/shard_map/ppermute | solution.py:83
  12.6 2.1 %reshape.111 = bf16[4096,64]{1,0:T(8,128)(2,1)S(1)} reshape(bf16[64,4096]{1,0:T(8,128)(2,1)} %param.12) | data formatting | bytes 1048576 | tf_op jit(solution)/shard_map/reshape | solution.py:31
  14.6 1.3 convolution_bitcast_fusion.1
  16.8 4.6 %fusion.46 = f32[64,64,64]{1,2,0:T(8,128)} fusion(f32[64,64,64]{1,0,2:T(8,128)S(1)} %reshape.112), kind=kOutput, calls=%fused_computation.59 | convolution fusion | flops 201383936 | bytes 2097152 | tf_op jit(solution)/shard_map/uy,pyw->puw/dot_general | solution.py:44
  21.4 4.7 %fusion.49 = f32[64,64,64]{1,2,0:T(8,128)} fusion(f32[64,64,64]{1,0,2:T(8,128)S(1)} %reshape.112), kind=kOutput, calls=%fused_computation.60 | convolution fusion | flops 201383936 | bytes 2097152 | tf_op jit(solution)/shard_map/uy,pyw->puw/dot_general | solution.py:47
  26.3 2.8 %multiply_reduce_fusion = (f32[64]{0:T(128)S(1)}, f32[64,64,32]{1,2,0:T(8,128)S(1)}, f32[64,64,32]{1,2,0:T(8,128)S(1)}) fusion(f32[64,32]{0,1:T(8,128)S(1)} %copy.44, f32[64,64,64]{1,2,0:T(8,128)} %fusion.49, f32[64,64,64]{1,2,0:T(8,128)} %fusion.46), kind=kLoop, calls=%fused_computation.65 | loop fusion | flops 1179584 | bytes 3154176 | tf_op jit(solution)/shard_map/reduce_sum | solution.py:71
  29.1 1.1 copy.39
  30.2 1.1 copy.40
  31.3 1.1 copy.41
  32.4 1.1 copy.42
  34.8 1.4 multiply_convert_fusion.1
  37.9 6.2 %collective-permute-done.1 = bf16[1,12,4096]{2,1,0:T(8,128)(2,1)S(1)} collective-permute-done((bf16[1,12,4096]{2,1,0:T(8,128)(2,1)S(1)}, bf16[1,12,4096]{2,1,0:T(8,128)(2,1)S(1)}, u32[]{:S(2)}, u32[]{:S(2)}) %collective-permute-start.1) | collective-permute-done | bytes 98336 | tf_op jit(solution)/shard_map/ppermute | solution.py:80
  45.0 25.9 %while.27 = (s32[]{:T(128)}, f32[64,384]{1,0:T(8,128)S(1)}, bf16[4,12,4096]{2,1,0:T(8,128)(2,1)}, bf16[64,4096]{1,0:T(8,128)(2,1)S(1)}, f32[128,2048]{1,0:T(8,12...) while((s32[]{:T(128)}, f32[64,384]{1,0:T(8,128)S(1)}, ...), condition=%wide.region_1.2_spmd.clone.clone, body=%wide.region_0.1_spmd.clone.clone.sunk | while | flops 92814080 | bytes 4696571 | solution.py:125
  46.0 1.1 fusion.137
  49.8 1.2 fusion.140
  56.2 1.2 fusion.140
  62.8 1.2 fusion.140
  69.3 1.2 fusion.140
  73.7 21.0 %while.28 = (s32[]{:T(128)}, f32[4,12,4096]{2,1,0:T(8,128)}, s32[4]{0:T(128)S(1)}, bf16[64,4,96]{0,2,1:T(8,128)(2,1)S(1)}, bf16[64,4096]{1,0:T(8,128)(2,1)S(1)},...) while((s32[]{:T(128)}, f32[4,12,4096]{2,1,0:T(8,128)}, ...), condition=%wide.region_9.10_spmd.clone.clone, body=%wide.region_6.9_spmd.clone.clone.sunk | while | flops 52166660 | bytes 4629223 | solution.py:165
  96.2 39.2 %all-reduce = (f32[4,128]{1,0:T(4,128)S(1)}, f32[]{:T(128)}) all-reduce(f32[4,128]{1,0:T(4,128)S(1)} %fusion.68, f32[]{:T(128)} %add_reduce_fusion.1), channel_id=1, replica_groups=mesh['gx'=4,'gy'=8] {'gx','gy'}, use_global_device_ids=true, to_apply=%region_13.14 | all-reduce | flops 513 | bytes 4104 | tf_op jit(solution)/shard_map/psum | solution.py:174
  135.4 1.2 fusion.54
  137.3 52.3 %all-reduce.3.cloned.1.call-done = f32[1,12,4096]{2,1,0:T(8,128)} async-done(((f32[1,12,4096]{2,1,0:T(8,128)}), f32[1,12,4096]{2,1,0:T(8,128)}) %all-reduce.3.cloned.1.call-update) | async-done | bytes 196624 | tf_op jit(solution)/shard_map/psum | solution.py:173
  189.6 1.8 copy.45
  (113 shorter events, 42.3 us)
Async XLA Ops:
  7.2 128.2 %reduce-scatter.2.cloned.1.call-start = ((), (), s32[]{:S(2)}) async-start(), calls=%async_computation.1 | async-start | bytes 1310720 | tf_op jit(solution)/shard_map/reduce_scatter | solution.py:164
  7.2 30.1 %collective-permute-start = (bf16[1,12,4096]{2,1,0:T(8,128)(2,1)}, bf16[1,12,4096]{2,1,0:T(8,128)(2,1)S(1)}, u32[]{:S(2)}, u32[]{:S(2)}) collective-permute-start(bf16[1,12,4096]{2,1,0:T(8,128)(2,1)} %param.13), channel_id=1, source_target_pairs={{0,8},{8,16},{16,24},{24,0},{1,9},{9,17},{17,25},{25,1},{2,10},{10... | collective-permute-start | bytes 294920 | tf_op jit(solution)/shard_map/ppermute | solution.py:80
  10.3 33.8 %collective-permute-start.2 = (bf16[1,12,4096]{2,1,0:T(8,128)(2,1)}, bf16[1,12,4096]{2,1,0:T(8,128)(2,1)S(1)}, u32[]{:S(2)}, u32[]{:S(2)}) collective-permute-start(bf16[1,12,4096]{2,1,0:T(8,128)(2,1)} %param.13), channel_id=1, source_target_pairs={{0,24},{8,0},{16,8},{24,16},{1,25},{9,1},{17,9},{25,17},{2,26},{10... | collective-permute-start | bytes 294920 | tf_op jit(solution)/shard_map/ppermute | solution.py:83
  21.4 4.7 %copy-start.4 = (f32[2048]{0:T(1024)S(1)}, f32[2048]{0:T(1024)}, u32[]{:S(2)}) copy-start(f32[2048]{0:T(1024)} %param.19) | copy-start | bytes 24580
  31.3 2.2 %copy-start = (f32[128,2048]{1,0:T(8,128)S(1)}, f32[128,2048]{1,0:T(8,128)}, u32[]{:S(2)}) copy-start(f32[128,2048]{1,0:T(8,128)} %param.18) | copy-start | bytes 3145732
  32.4 1.3 copy-start.6
  32.4 2.4 %copy-start.1 = (f32[64,2048]{1,0:T(8,128)S(1)}, f32[64,2048]{1,0:T(8,128)}, u32[]{:S(2)}) copy-start(f32[64,2048]{1,0:T(8,128)} %copy.40) | copy-start | bytes 1572868
  33.5 1.3 copy-start.2
  33.6 2.7 %copy-start.7 = (f32[4]{0:T(128)S(1)}, f32[4]{0:T(128)}, u32[]{:S(2)}) copy-start(f32[4]{0:T(128)} %param.15) | copy-start | bytes 52
  33.7 2.7 %copy-start.8 = (s32[4]{0:T(128)S(1)}, s32[4]{0:T(128)}, u32[]{:S(2)}) copy-start(s32[4]{0:T(128)} %param.14) | copy-start | bytes 52
  34.8 9.2 %copy-start.3 = (bf16[1,12,4096]{2,1,0:T(8,128)(2,1)S(1)}, bf16[1,12,4096]{2,1,0:T(8,128)(2,1)}, u32[]{:S(2)}) copy-start(bf16[1,12,4096]{2,1,0:T(8,128)(2,1)} %param.13) | copy-start | bytes 294916
  36.5 0.7 copy-start.5
  37.3 6.8 %collective-permute-start.1 = (bf16[1,12,4096]{2,1,0:T(8,128)(2,1)S(1)}, bf16[1,12,4096]{2,1,0:T(8,128)(2,1)S(1)}, u32[]{:S(2)}, u32[]{:S(2)}) collective-permute-start(bf16[1,12,4096]{2,1,0:T(8,128)(2,1)S(1)} %collective-permute-done), channel_id=1, source_target_pairs={{0,8},{8,16},{16,24},{24,0},{1,9},{9,17},{17,25},{25,1},{2,10},{10... | collective-permute-start | bytes 294920 | tf_op jit(solution)/shard_map/ppermute | solution.py:80
  94.7 94.9 %all-reduce.3.cloned.1.call-start = ((), (), s32[]{:S(2)}) async-start(), calls=%async_computation.2 | async-start | bytes 524288 | tf_op jit(solution)/shard_map/psum | solution.py:173
Sparse Core Ops, SparseCore 0:
  94.8 26.3 reduce-scatter.1
  135.6 53.9 all-reduce.2
